TPU v7x, 128 devices: a whole 4x4x4 slice. The times are simulated.
128 devices in a mesh: sec: 2 (over z_lo), row: 8 (over x, z_hi), col: 8 (over y, core).
Axes of the slice: x: 4, y: 4, z: 4 (z_hi: 2, z_lo: 2; z = z_hi * 2 + z_lo), core: 2. Of those that a mesh axis runs over, the one named last changes fastest.
Arguments:
- held_inverse: bfloat16 [12288, 12288], P('row', ('sec', 'col')), as said below
- factor_panels: bfloat16 [2, 12288, 1024], P(None, ('sec', 'col'), 'row'), may hold values from -0.125 to 0.125
- block_inverses: bfloat16 [2, 1024, 1024], P(None, 'row'), as said below
- covariance: float32 [12288, 12288], P('row', ('sec', 'col')), may hold values from -0.9 to 0.9
Outputs:
- updated: float32 [12288, 12288], P('row', ('sec', 'col'))
Inputs may be any that keep to these rules, and one draw needn't show every extreme that they name: held_inverse is lower triangular with a positive diagonal. Each block of block_inverses is lower triangular with a positive diagonal.
All inputs are finite; a program needn't handle non-finite values.
Results may differ from a plain program's by a relative error of at most 0.0038.
Values may be sent and summed in bfloat16 or wider, within the bound.
A program may use at most 128 MiB of HBM per device.

v0:
```python
import jax
import jax.numpy as jnp
from jax import lax
from jax.sharding import Mesh
from jax.sharding import PartitionSpec as P

PANELS = 2
ROW = ("row_0", "row_1")


def scatter_axes(x, axes, dim):
    for axis in axes:
        x = lax.psum_scatter(x, axis, scatter_dimension=dim, tiled=True)
    return x


def from_root(x, axis, root):
    mine = lax.axis_index(axis) == root
    return lax.psum(jnp.where(mine, x, jnp.zeros_like(x)), axis)


def body(held_inverse, factor_panels, block_inverses, covariance):
    total = covariance
    tile_cols = held_inverse.shape[1]
    groups = lax.axis_size(("sec", "col"))
    ratio = groups // lax.axis_size(ROW)
    column_index = lax.axis_index(("sec", "col"))
    root_row = column_index // ratio
    offset = column_index % ratio * tile_cols
    for panel in range(PANELS):
        partial_value = jnp.dot(
            factor_panels[panel], block_inverses[panel], preferred_element_type=jnp.float32
        )
        scaled = scatter_axes(partial_value, ROW, 1).astype(jnp.bfloat16)
        terms = jnp.dot(
            held_inverse,
            lax.all_gather(scaled, ROW, axis=1, tiled=True),
            preferred_element_type=jnp.float32,
        )
        summed = lax.psum(terms, ("sec", "col"))
        inverse = (-summed).astype(jnp.bfloat16)
        own_block = lax.dynamic_slice_in_dim(inverse, offset, tile_cols, 0)
        column_block = from_root(own_block, ROW, root_row)
        total = total + lax.dot_general(
            inverse, column_block, (((1,), (1,)), ((), ())), preferred_element_type=jnp.float32
        )
    return total


def solution(mesh):
    split = Mesh(
        mesh.devices.reshape(mesh.shape["sec"], 4, 2, mesh.shape["col"]),
        ("sec", "row_0", "row_1", "col"),
    )
    in_specs = (
        P(ROW, ("sec", "col")),
        P(None, ("sec", "col"), ROW),
        P(None, ROW, None),
        P(ROW, ("sec", "col")),
    )
    out_specs = P(ROW, ("sec", "col"))
    return jax.shard_map(body, mesh=split, in_specs=in_specs, out_specs=out_specs, check_vma=False)
```

profile of v0, /device:TPU:5, one launch (start us, length us, event | category | flops | bytes accessed | tf_op | source)
XLA Modules:
  0.0 585.9 jit_solution(17937898365134801965)
XLA Ops:
  6.5 3.4 fusion.2
  10.0 0.0 reduce-scatter.9.cloned.1.call-start
  10.1 2.2 fusion
  12.3 36.8 %reduce-scatter.5.cloned.1.call-done = f32[768,256]{1,0:T(8,128)} async-done(((f32[768,1024]{1,0:T(8,128)}), f32[768,256]{1,0:T(8,128)}) %reduce-scatter.5.cloned.1.call-update) | async-done | bytes 786448 | tf_op jit(solution)/shard_map/reduce_scatter | solution.py:13
  49.2 40.3 %reduce-scatter.9.cloned.1.call-done = f32[768,256]{1,0:T(8,128)} async-done(((f32[768,1024]{1,0:T(8,128)}), f32[768,256]{1,0:T(8,128)}) %reduce-scatter.9.cloned.1.call-update) | async-done | bytes 786448 | tf_op jit(solution)/shard_map/reduce_scatter | solution.py:13
  89.6 25.2 %reduce-scatter.7.cloned.1.call-done = f32[768,128]{1,0:T(8,128)} async-done(((f32[768,256]{1,0:T(8,128)}), f32[768,128]{1,0:T(8,128)}) %reduce-scatter.7.cloned.1.call-update) | async-done | bytes 393232 | tf_op jit(solution)/shard_map/reduce_scatter | solution.py:13
  114.8 1.7 convert_element_type.12
  116.6 0.0 all-gather.5.cloned.1.call-start
  116.6 21.3 %reduce-scatter.11.cloned.1.call-done = f32[768,128]{1,0:T(8,128)} async-done(((f32[768,256]{1,0:T(8,128)}), f32[768,128]{1,0:T(8,128)}) %reduce-scatter.11.cloned.1.call-update) | async-done | bytes 393232 | tf_op jit(solution)/shard_map/reduce_scatter | solution.py:13
  138.0 1.7 convert_element_type.14
  139.7 0.0 all-reduce.5.cloned.1.call-start
  139.7 49.3 %all-gather.3.cloned.1.call-done = bf16[768,1024]{1,0:T(8,128)(2,1)} async-done(((bf16[768,128]{1,0:T(8,128)(2,1)}), bf16[768,1024]{1,0:T(8,128)(2,1)}) %all-gather.3.cloned.1.call-update) | async-done | bytes 1572880 | tf_op jit(solution)/shard_map/all_gather | solution.py:37
  189.0 6.1 %convolution_bitcast_fusion.1 = f32[1536,1024]{0,1:T(8,128)} fusion(bf16[768,1024]{1,0:T(8,128)(2,1)} %all-gather.3.cloned.1.call-done, bf16[1536,768]{1,0:T(8,128)(2,1)S(1)} %copy-done), kind=kOutput, calls=%fused_computation.4 | convolution fusion | flops 2415919104 | bytes 10223616 | tf_op jit(solution)/shard_map/dot_general | solution.py:35
  195.2 47.0 %all-gather.5.cloned.1.call-done = bf16[768,1024]{1,0:T(8,128)(2,1)} async-done(((bf16[768,128]{1,0:T(8,128)(2,1)}), bf16[768,1024]{1,0:T(8,128)(2,1)}) %all-gather.5.cloned.1.call-update) | async-done | bytes 1572880 | tf_op jit(solution)/shard_map/all_gather | solution.py:37
  242.1 6.0 %convolution_bitcast_fusion = f32[1536,1024]{0,1:T(8,128)} fusion(bf16[768,1024]{1,0:T(8,128)(2,1)} %all-gather.5.cloned.1.call-done, bf16[1536,768]{1,0:T(8,128)(2,1)S(1)} %copy-done), kind=kOutput, calls=%fused_computation.3 | convolution fusion | flops 2415919104 | bytes 10223616 | tf_op jit(solution)/shard_map/dot_general | solution.py:35
  248.1 0.0 all-reduce.7.cloned.1.call-start
  248.2 159.2 %all-reduce.5.cloned.1.call-done = (f32[1536,1024]{0,1:T(8,128)}, f32[1536,1024]{0,1:T(8,128)}) async-done(((f32[1536,1024]{0,1:T(8,128)}, f32[1536,1024]{0,1:T(8,128)}), (f32[1536,1024]{0,1:T(8,128)}, f32[1536,1024]{0,1:T(8,128)})) %all-reduce.5.cloned.1.call-update) | async-done | bytes 12582928 | tf_op jit(solution)/shard_map/psum | solution.py:40
  407.4 6.3 %negate_convert_fusion = (bf16[1536,1024]{0,1:T(8,128)(2,1)S(1)}, bf16[1536,1024]{0,1:T(8,128)(2,1)S(1)}) fusion(f32[1536,1024]{0,1:T(8,128)} %get-tuple-element.6, f32[1536,1024]{0,1:T(8,128)} %get-tuple-element.5), kind=kLoop, calls=%fused_computation | loop fusion | flops 6291456 | bytes 18874368 | tf_op jit(solution)/shard_map/convert_element_type | solution.py:41
  413.7 1.7 dynamic-slice_select_fusion.1
  415.4 0.4 copy-done.2
  415.9 1.5 dynamic-slice_select_fusion
  417.4 151.0 %all-reduce.7.cloned.1.call-done = (bf16[768,1024]{0,1:T(8,128)(2,1)}, bf16[768,1024]{0,1:T(8,128)(2,1)}) async-done(((bf16[768,1024]{0,1:T(8,128)(2,1)}, bf16[768,1024]{0,1:T(8,128)(2,1)}), (bf16[768,1024]{0,1:T(8,128)(2,1)}, bf16[768,1024]{0,1:T(8,128)(2,1)})) %all-reduce.7.cloned.1.call-update) | async-done | bytes 3145744 | tf_op jit(solution)/shard_map/psum | solution.py:19
  568.4 4.3 fusion.10
  572.7 6.4 %add_add_fusion = f32[1536,768]{1,0:T(8,128)} fusion(f32[1536,768]{1,0:T(8,128)} %param.7, f32[1536,768]{1,0:T(8,128)S(1)} %fusion.10, bf16[1536,1024]{0,1:T(8,128)(2,1)S(1)} %copy-done.3, bf16[768,1024]{0,1:T(8,128)(2,1)S(1)} %copy-done.6), kind=kOutput, calls=%fused_computation.2 | convolution fusion | flops 2418278400 | bytes 18874368 | tf_op jit(solution)/shard_map/dot_general | solution.py:44
  (25 shorter events, 0.3 us)
Async XLA Ops:
  6.5 182.5 %copy-start = (bf16[1536,768]{1,0:T(8,128)(2,1)S(1)}, bf16[1536,768]{1,0:T(8,128)(2,1)}, u32[]{:S(2)}) copy-start(bf16[1536,768]{1,0:T(8,128)(2,1)} %param.4) | copy-start | bytes 7077892
  6.5 3.5 copy-start.4
  6.5 3.5 copy-start.5
  6.5 42.6 %reduce-scatter.5.cloned.1.call-start = ((), (), s32[]{:S(2)}) async-start(), calls=%async_computation.4 | async-start | bytes 3932160 | tf_op jit(solution)/shard_map/reduce_scatter | solution.py:13
  10.0 79.6 %reduce-scatter.9.cloned.1.call-start = ((), (), s32[]{:S(2)}) async-start(), calls=%async_computation.7 | async-start | bytes 3932160 | tf_op jit(solution)/shard_map/reduce_scatter | solution.py:13
  12.3 102.6 %reduce-scatter.7.cloned.1.call-start = ((), (), s32[]{:S(2)}) async-start(), calls=%async_computation.5 | async-start | bytes 1179648 | tf_op jit(solution)/shard_map/reduce_scatter | solution.py:13
  49.2 88.8 %reduce-scatter.11.cloned.1.call-start = ((), (), s32[]{:S(2)}) async-start(), calls=%async_computation.8 | async-start | bytes 1179648 | tf_op jit(solution)/shard_map/reduce_scatter | solution.py:13
  89.6 99.4 %all-gather.3.cloned.1.call-start = ((), (), s32[]{:S(2)}) async-start(), calls=%async_computation.6 | async-start | bytes 1769472 | tf_op jit(solution)/shard_map/all_gather | solution.py:37
  116.6 125.6 %all-gather.5.cloned.1.call-start = ((), (), s32[]{:S(2)}) async-start(), calls=%async_computation.9 | async-start | bytes 1769472 | tf_op jit(solution)/shard_map/all_gather | solution.py:37
  139.7 267.7 %all-reduce.5.cloned.1.call-start = ((), (), s32[]{:S(2)}) async-start(), calls=%async_computation.10 | async-start | bytes 25165824 | tf_op jit(solution)/shard_map/psum | solution.py:40
  248.1 320.3 %all-reduce.7.cloned.1.call-start = ((), (), s32[]{:S(2)}) async-start(), calls=%async_computation.11 | async-start | bytes 6291456 | tf_op jit(solution)/shard_map/psum | solution.py:19
  413.7 2.2 copy-start.2
  568.4 4.3 copy-start.3
  568.4 4.3 copy-start.6
  572.7 6.4 %copy-start.1 = (bf16[1536,768]{1,0:T(8,128)(2,1)S(1)}, bf16[1536,768]{1,0:T(8,128)(2,1)}, u32[]{:S(2)}) copy-start(bf16[1536,768]{1,0:T(8,128)(2,1)} %param.4) | copy-start | bytes 7077892
Sparse Core Ops, SparseCore 0:
  10.1 38.9 reduce-scatter.4
  51.6 37.9 reduce-scatter.8
  91.9 22.8 reduce-scatter.6
  117.0 20.8 reduce-scatter.10
  140.0 48.9 all-gather.2
  191.0 51.0 all-gather.4
  248.2 159.1 all-reduce.4
  417.5 150.8 all-reduce.6
where the time goes:
time: 586 us
  waiting for transfers between devices  530 us (90%)
  matrix products  28.4 us (5%)
  between operations  13.6 us (2%)
  other arithmetic  12.9 us (2%)
    psum x1, waiting for transfers between devices, body(): summed = lax.psum(terms, ('sec', 'col'))  159 us
    psum x1, waiting for transfers between devices, from_root(): return lax.psum(jnp.where(mine, x, jnp.zeros_like(x)), axis)  151 us
    reduce_scatter x4, waiting for transfers between devices, scatter_axes(): x = lax.psum_scatter(x, axis, scatter_dimension=dim, tiled=True)  124 us
    all_gather x2, waiting for transfers between devices, body(): lax.all_gather(scaled, ROW, axis=1, tiled=True)  96.2 us
    dot_general x2, matrix products, body(): jnp.dot(held_inverse, lax.all_gather(scaled, ROW, axis=1, tiled=True), pr...  12.1 us
  transfers between devices with their start and end apart: 8, of which 8 were waited for; matrix products, arithmetic and copies ran while one was open for 2% of the time, Pallas kernels for 0%

commit v1 on v0

--- a/solution.py
+++ b/solution.py
@@ -37,7 +37,8 @@
             lax.all_gather(scaled, ROW, axis=1, tiled=True),
             preferred_element_type=jnp.float32,
         )
-        summed = lax.psum(terms, ("sec", "col"))
+        half = lax.psum(terms, "sec")
+        summed = lax.psum(half, "col")
         inverse = (-summed).astype(jnp.bfloat16)
         own_block = lax.dynamic_slice_in_dim(inverse, offset, tile_cols, 0)
         column_block = from_root(own_block, ROW, root_row)

time: 586 us -> 869 us (1.48)
  waiting for transfers between devices: 530 us -> 814 us
    psum x1 -> x2, waiting for transfers between devices: 159 us -> 443 us  [the longest x1 296 us: body(): half = lax.psum(terms, 'sec')]
  transfers between devices with their start and end apart: 8 -> 9, of which waited for: 8 -> 9; matrix products, arithmetic and copies ran while one was open for 2% -> 1% of each run, Pallas kernels for 0% -> 0%
where the time goes in v1:
time: 869 us
  waiting for transfers between devices  814 us (94%)
  matrix products  28.4 us (3%)
  between operations  13.3 us (2%)
  other arithmetic  12.9 us (1%)
    psum x1, waiting for transfers between devices, body(): half = lax.psum(terms, 'sec')  296 us
    psum x1, waiting for transfers between devices, from_root(): return lax.psum(jnp.where(mine, x, jnp.zeros_like(x)), axis)  150 us
    psum x1, waiting for transfers between devices, body(): summed = lax.psum(half, 'col')  147 us
    reduce_scatter x4, waiting for transfers between devices, scatter_axes(): x = lax.psum_scatter(x, axis, scatter_dimension=dim, tiled=True)  124 us
    all_gather x2, waiting for transfers between devices, body(): lax.all_gather(scaled, ROW, axis=1, tiled=True)  96.3 us
  transfers between devices with their start and end apart: 9, of which 9 were waited for; matrix products, arithmetic and copies ran while one was open for 1% of the time, Pallas kernels for 0%

profile of v1, /device:TPU:5, one launch (start us, length us, event | category | flops | bytes accessed | tf_op | source)
XLA Modules:
  0.0 869.0 jit_solution(7928242597934804811)
XLA Ops:
  6.5 3.4 fusion.2
  10.0 0.0 reduce-scatter.9.cloned.1.call-start
  10.1 2.2 fusion
  12.3 36.8 %reduce-scatter.5.cloned.1.call-done = f32[768,256]{1,0:T(8,128)} async-done(((f32[768,1024]{1,0:T(8,128)}), f32[768,256]{1,0:T(8,128)}) %reduce-scatter.5.cloned.1.call-update) | async-done | bytes 786448 | tf_op jit(solution)/shard_map/reduce_scatter | solution.py:13
  49.2 40.3 %reduce-scatter.9.cloned.1.call-done = f32[768,256]{1,0:T(8,128)} async-done(((f32[768,1024]{1,0:T(8,128)}), f32[768,256]{1,0:T(8,128)}) %reduce-scatter.9.cloned.1.call-update) | async-done | bytes 786448 | tf_op jit(solution)/shard_map/reduce_scatter | solution.py:13
  89.6 25.2 %reduce-scatter.7.cloned.1.call-done = f32[768,128]{1,0:T(8,128)} async-done(((f32[768,256]{1,0:T(8,128)}), f32[768,128]{1,0:T(8,128)}) %reduce-scatter.7.cloned.1.call-update) | async-done | bytes 393232 | tf_op jit(solution)/shard_map/reduce_scatter | solution.py:13
  114.8 1.7 convert_element_type.12
  116.6 0.0 all-gather.5.cloned.1.call-start
  116.6 21.3 %reduce-scatter.11.cloned.1.call-done = f32[768,128]{1,0:T(8,128)} async-done(((f32[768,256]{1,0:T(8,128)}), f32[768,128]{1,0:T(8,128)}) %reduce-scatter.11.cloned.1.call-update) | async-done | bytes 393232 | tf_op jit(solution)/shard_map/reduce_scatter | solution.py:13
  138.0 1.7 convert_element_type.14
  139.7 0.0 all-reduce.9.cloned.1.call-start
  139.7 49.3 %all-gather.3.cloned.1.call-done = bf16[768,1024]{1,0:T(8,128)(2,1)} async-done(((bf16[768,128]{1,0:T(8,128)(2,1)}), bf16[768,1024]{1,0:T(8,128)(2,1)}) %all-gather.3.cloned.1.call-update) | async-done | bytes 1572880 | tf_op jit(solution)/shard_map/all_gather | solution.py:37
  189.0 6.0 convolution_bitcast_fusion.1
  195.0 47.1 %all-gather.5.cloned.1.call-done = bf16[768,1024]{1,0:T(8,128)(2,1)} async-done(((bf16[768,128]{1,0:T(8,128)(2,1)}), bf16[768,1024]{1,0:T(8,128)(2,1)}) %all-gather.5.cloned.1.call-update) | async-done | bytes 1572880 | tf_op jit(solution)/shard_map/all_gather | solution.py:37
  242.1 6.1 convolution_bitcast_fusion
  248.3 296.2 %all-reduce.9.cloned.1.call-done = (f32[1536,1024]{0,1:T(8,128)}, f32[1536,1024]{0,1:T(8,128)}) async-done(((f32[1536,1024]{0,1:T(8,128)}, f32[1536,1024]{0,1:T(8,128)}), (f32[1536,1024]{0,1:T(8,128)}, f32[1536,1024]{0,1:T(8,128)})) %all-reduce.9.cloned.1.call-update) | async-done | bytes 12582928 | tf_op jit(solution)/shard_map/psum | solution.py:40
  544.5 146.9 %all-reduce.7.cloned.1.call-done = (f32[1536,1024]{0,1:T(8,128)}, f32[1536,1024]{0,1:T(8,128)}) async-done(((f32[1536,1024]{0,1:T(8,128)}, f32[1536,1024]{0,1:T(8,128)}), (f32[1536,1024]{0,1:T(8,128)}, f32[1536,1024]{0,1:T(8,128)})) %all-reduce.7.cloned.1.call-update) | async-done | bytes 12582928 | tf_op jit(solution)/shard_map/psum | solution.py:41
  691.5 6.3 negate_convert_fusion
  697.8 1.7 dynamic-slice_select_fusion.1
  699.5 0.4 copy-done.2
  700.0 1.5 dynamic-slice_select_fusion
  701.5 150.2 %all-reduce.11.cloned.1.call-done = (bf16[768,1024]{0,1:T(8,128)(2,1)}, bf16[768,1024]{0,1:T(8,128)(2,1)}) async-done(((bf16[768,1024]{0,1:T(8,128)(2,1)}, bf16[768,1024]{0,1:T(8,128)(2,1)}), (bf16[768,1024]{0,1:T(8,128)(2,1)}, bf16[768,1024]{0,1:T(8,128)(2,1)})) %all-reduce.11.cloned.1.call-update) | async-done | bytes 3145744 | tf_op jit(solution)/shard_map/psum | solution.py:19
  851.7 4.3 fusion.10
  856.1 6.3 add_add_fusion
  (28 shorter events, 0.4 us)
Async XLA Ops:
  6.5 182.5 %copy-start = (bf16[1536,768]{1,0:T(8,128)(2,1)S(1)}, bf16[1536,768]{1,0:T(8,128)(2,1)}, u32[]{:S(2)}) copy-start(bf16[1536,768]{1,0:T(8,128)(2,1)} %param.4) | copy-start | bytes 7077892
  6.5 3.5 copy-start.4
  6.5 3.5 copy-start.5
  6.5 42.6 %reduce-scatter.5.cloned.1.call-start = ((), (), s32[]{:S(2)}) async-start(), calls=%async_computation.4 | async-start | bytes 3932160 | tf_op jit(solution)/shard_map/reduce_scatter | solution.py:13
  10.0 79.6 %reduce-scatter.9.cloned.1.call-start = ((), (), s32[]{:S(2)}) async-start(), calls=%async_computation.7 | async-start | bytes 3932160 | tf_op jit(solution)/shard_map/reduce_scatter | solution.py:13
  12.3 102.6 %reduce-scatter.7.cloned.1.call-start = ((), (), s32[]{:S(2)}) async-start(), calls=%async_computation.5 | async-start | bytes 1179648 | tf_op jit(solution)/shard_map/reduce_scatter | solution.py:13
  49.2 88.8 %reduce-scatter.11.cloned.1.call-start = ((), (), s32[]{:S(2)}) async-start(), calls=%async_computation.8 | async-start | bytes 1179648 | tf_op jit(solution)/shard_map/reduce_scatter | solution.py:13
  89.6 99.4 %all-gather.3.cloned.1.call-start = ((), (), s32[]{:S(2)}) async-start(), calls=%async_computation.6 | async-start | bytes 1769472 | tf_op jit(solution)/shard_map/all_gather | solution.py:37
  116.6 125.6 %all-gather.5.cloned.1.call-start = ((), (), s32[]{:S(2)}) async-start(), calls=%async_computation.9 | async-start | bytes 1769472 | tf_op jit(solution)/shard_map/all_gather | solution.py:37
  139.7 404.8 %all-reduce.9.cloned.1.call-start = ((), (), s32[]{:S(2)}) async-start(), calls=%async_computation.11 | async-start | bytes 25165824 | tf_op jit(solution)/shard_map/psum | solution.py:40
  248.2 443.3 %all-reduce.7.cloned.1.call-start = ((), (), s32[]{:S(2)}) async-start(), calls=%async_computation.10 | async-start | bytes 25165824 | tf_op jit(solution)/shard_map/psum | solution.py:41
  544.5 307.2 %all-reduce.11.cloned.1.call-start = ((), (), s32[]{:S(2)}) async-start(), calls=%async_computation.12 | async-start | bytes 6291456 | tf_op jit(solution)/shard_map/psum | solution.py:19
  697.8 2.2 copy-start.2
  851.7 4.3 copy-start.3
  851.7 4.3 copy-start.6
  856.1 6.4 copy-start.1
Sparse Core Ops, SparseCore 0:
  10.1 38.9 reduce-scatter.4
  51.6 37.9 reduce-scatter.8
  91.9 22.8 reduce-scatter.6
  117.0 20.8 reduce-scatter.10
  140.0 48.9 all-gather.2
  191.0 51.0 all-gather.4
  248.3 296.0 all-reduce.8
  546.9 144.5 all-reduce.6
  701.6 150.0 all-reduce.10
